TPU v7x, 512 devices: a whole 4x4x16 slice. The times are simulated.
512 devices in a mesh: factor: 16 (over x_hi, y, core), load: 32 (over z, x_lo).
Axes of the slice: x: 4 (x_hi: 2, x_lo: 2; x = x_hi * 2 + x_lo), y: 4, z: 16, core: 2. Of those that a mesh axis runs over, the one named last changes fastest.
Arguments:
- b_panel: bfloat16 [2048, 8192], P('factor', 'load'), may hold values from -6 to 6
- b_update: bfloat16 [8192, 8192], P('factor', 'load'), may hold values from -6 to 6
- panel_inverse: bfloat16 [2048, 2048], P('factor'), as said below
- update_factor: bfloat16 [8192, 2048], P('factor'), may hold values from -0.125 to 0.125
- update_solution: bfloat16 [8192, 8192], P(('factor', 'load')), may hold values from -3 to 3
- axle_weights: bfloat16 [3072, 8192], P('load'), may hold values from -0.0625 to 0.0625
Outputs:
- update_rhs: bfloat16 [8192, 8192], P('factor', 'load')
- panel_solution: bfloat16 [2048, 8192], P('factor', 'load')
- config_response: float32 [3072, 2048], P('load', 'factor')
Inputs may be any that keep to these rules, and one draw needn't show every extreme that they name: panel_inverse is zero above the diagonal and its diagonal lies between 1 and 2.
All inputs are finite; a program needn't handle non-finite values.
Results may differ from a plain program's by a relative error of at most 0.0052.
Values may be sent and summed in bfloat16 or wider, within the bound.
A program may use at most 64 MiB of HBM per device.

v0:
```python
import jax
import jax.numpy as jnp
from jax import lax
from jax.sharding import PartitionSpec as P


def local(b_panel, b_update, panel_inverse, update_factor, update_solution, axle_weights):
    block = panel_inverse
    forward = jnp.dot(
        block,
        lax.all_gather(b_panel, "factor", axis=0, tiled=True),
        preferred_element_type=jnp.float32,
    ).astype(jnp.bfloat16)
    block = update_factor
    lowered = jnp.dot(
        block,
        lax.all_gather(forward, "factor", axis=0, tiled=True),
        preferred_element_type=jnp.float32,
    )
    update_rhs = (b_update.astype(jnp.float32) - lowered).astype(jnp.bfloat16)
    regrouped = lax.all_to_all(update_solution, "load", split_axis=1, concat_axis=0, tiled=True)
    factor_cols = lax.all_to_all(update_factor, "factor", split_axis=1, concat_axis=0, tiled=True)
    block = factor_cols
    coupled = lax.dot_general(
        block,
        lax.all_gather(regrouped, "factor", axis=0, tiled=True),
        (((0,), (0,)), ((), ())),
        preferred_element_type=jnp.float32,
    )
    reduced = (forward.astype(jnp.float32) - coupled).astype(jnp.bfloat16)
    block = panel_inverse
    panel_solution = lax.psum_scatter(
        lax.dot_general(
            block, reduced, (((0,), (0,)), ((), ())), preferred_element_type=jnp.float32
        ),
        "factor",
        scatter_dimension=0,
        tiled=True,
    ).astype(jnp.bfloat16)
    block = axle_weights
    config_response = lax.dot_general(
        block,
        lax.all_gather(panel_solution, "load", axis=1, tiled=True),
        (((1,), (1,)), ((), ())),
        preferred_element_type=jnp.float32,
    )
    return (update_rhs, panel_solution, config_response)


def solution(mesh):
    in_specs = (
        P("factor", "load"),
        P("factor", "load"),
        P("factor", None),
        P("factor", None),
        P(("factor", "load"), None),
        P("load", None),
    )
    out_specs = (P("factor", "load"), P("factor", "load"), P("load", "factor"))
    return jax.shard_map(local, mesh=mesh, in_specs=in_specs, out_specs=out_specs, check_vma=False)
```

profile of v0, /device:TPU:24, one launch (start us, length us, event | category | flops | bytes accessed | tf_op | source)
XLA Modules:
  0.0 457.6 jit_solution(6282745598450169393)
XLA Ops:
  7.2 0.0 copy-start
  7.2 0.0 all-gather.5.cloned.1.call-start
  7.2 0.7 all-gather.5.cloned.1.call-update
  7.9 0.0 all-gather.9.cloned.1.call-start
  8.0 1.0 copy.29
  8.9 38.2 %all_to_all.38 = bf16[16,32,256]{2,0,1:T(8,128)(2,1)} all-to-all(bf16[16,32,256]{2,0,1:T(8,128)(2,1)S(1)} %bitcast.33), channel_id=1, replica_groups=mesh['factor'=16,'load'=32] {'load'}, dimensions={1} | all-to-all | bytes 524288 | tf_op jit(solution)/shard_map/all_to_all | solution.py:21
  47.1 0.0 all-gather.9.cloned.1.call-update
  47.2 0.0 reduce-scatter.2.cloned.1.call-start
  47.2 3.9 copy.22
  51.1 36.8 %all_to_all.39 = bf16[512,16,128]{0,2,1:T(8,128)(2,1)} all-to-all(bf16[512,16,128]{0,2,1:T(8,128)(2,1)} %bitcast.31), channel_id=1, replica_groups=mesh['factor'=16,'load'=32] {'factor'}, dimensions={1} | all-to-all | bytes 4194304 | tf_op jit(solution)/shard_map/all_to_all | solution.py:22
  88.0 4.0 copy.23
  92.0 0.0 copy-done.1
  92.0 1.5 convolution_convert_fusion
  93.5 0.0 copy-start.2
  93.5 56.7 %all-gather.9.cloned.1.call-done = bf16[8192,256]{1,0:T(8,128)(2,1)} async-done(((bf16[512,256]{1,0:T(8,128)(2,1)}), bf16[8192,256]{1,0:T(8,128)(2,1)}) %all-gather.9.cloned.1.call-update) | async-done | bytes 4194320 | tf_op jit(solution)/shard_map/all_gather | solution.py:26
  150.2 5.9 %convolution_bitcast_fusion = f32[2048,256]{0,1:T(8,128)} fusion(bf16[128,2048]{1,0:T(8,128)(2,1)S(1)} %copy-done.1, bf16[8192,128]{1,0:T(8,128)(2,1)} %bitcast.29, bf16[8192,256]{1,0:T(8,128)(2,1)} %all-gather.9.cloned.1.call-done, bf16[128,256]{1,0:T(8,128)(2,1)S(1)} %convolution_convert_fusion), kind=kOutput, calls=%fused_computation | convolution fusion | flops 671186944 | bytes 8978432 | tf_op jit(solution)/shard_map/dot_general | solution.py:33
  156.1 0.0 copy-done.2
  156.1 0.0 reduce-scatter.2.cloned.1.call-update
  156.1 0.0 all-gather.7.cloned.1.call-start
  156.2 0.5 all-gather.7.cloned.1.call-update
  156.7 0.0 all-gather.11.cloned.1.call-start
  156.8 92.8 %reduce-scatter.2.cloned.1.call-done = f32[128,256]{0,1:T(8,128)} async-done(((f32[2048,256]{0,1:T(8,128)}), f32[128,256]{0,1:T(8,128)}) %reduce-scatter.2.cloned.1.call-update) | async-done | bytes 131088 | tf_op jit(solution)/shard_map/reduce_scatter | solution.py:32
  249.6 1.5 convert_element_type.23
  251.1 0.0 all-gather.11.cloned.1.call-update
  251.1 0.0 copy-done.4
  251.1 0.1 copy.21
  251.3 61.9 %all-gather.7.cloned.1.call-done = bf16[2048,256]{1,0:T(8,128)(2,1)} async-done(((bf16[128,256]{1,0:T(8,128)(2,1)}), bf16[2048,256]{1,0:T(8,128)(2,1)}) %all-gather.7.cloned.1.call-update) | async-done | bytes 1048592 | tf_op jit(solution)/shard_map/all_gather | solution.py:17
  313.1 2.7 fusion.1
  315.8 0.8 copy.25
  316.7 0.7 copy.26
  317.4 130.8 %all-gather.11.cloned.1.call-done = bf16[128,8192]{0,1:T(8,128)(2,1)} async-done(((bf16[128,256]{0,1:T(8,128)(2,1)}), bf16[128,8192]{0,1:T(8,128)(2,1)}) %all-gather.11.cloned.1.call-update) | async-done | bytes 2097168 | tf_op jit(solution)/shard_map/all_gather | solution.py:43
  448.2 2.8 convolution_bitcast_fusion.2
  (6 shorter events, 0.0 us)
Async XLA Ops:
  7.2 441.1 %copy-start = (bf16[96,8192]{1,0:T(8,128)(2,1)S(1)}, bf16[96,8192]{1,0:T(8,128)(2,1)}, u32[]{:S(2)}) copy-start(bf16[96,8192]{1,0:T(8,128)(2,1)} %param.11) | copy-start | bytes 4718596
  7.2 84.8 %all-gather.5.cloned.1.call-start = ((), (), s32[]{:S(2)}) async-start(), calls=%async_computation.3 | async-start | bytes 1114112 | tf_op jit(solution)/shard_map/all_gather | solution.py:11
  7.9 142.3 %all-gather.9.cloned.1.call-start = ((), (), s32[]{:S(2)}) async-start(), calls=%async_computation.5 | async-start | bytes 4456448 | tf_op jit(solution)/shard_map/all_gather | solution.py:26
  47.2 202.4 %reduce-scatter.2.cloned.1.call-start = ((), (), s32[]{:S(2)}) async-start(), calls=%async_computation.6 | async-start | bytes 2228224 | tf_op jit(solution)/shard_map/reduce_scatter | solution.py:32
  88.0 4.0 copy-start.1
  93.5 62.6 %copy-start.2 = (bf16[128,256]{1,0:T(8,128)(2,1)}, bf16[128,256]{1,0:T(8,128)(2,1)S(1)}, u32[]{:S(2)}) copy-start(bf16[128,256]{1,0:T(8,128)(2,1)S(1)} %convolution_convert_fusion) | copy-start | bytes 196612
  156.1 95.0 %copy-start.4 = (bf16[512,256]{1,0:T(8,128)(2,1)S(1)}, bf16[512,256]{1,0:T(8,128)(2,1)}, u32[]{:S(2)}) copy-start(bf16[512,256]{1,0:T(8,128)(2,1)} %param.7) | copy-start | bytes 786436
  156.1 157.0 %all-gather.7.cloned.1.call-start = ((), (), s32[]{:S(2)}) async-start(), calls=%async_computation.4 | async-start | bytes 1114112 | tf_op jit(solution)/shard_map/all_gather | solution.py:17
  156.7 291.5 %all-gather.11.cloned.1.call-start = ((), (), s32[]{:S(2)}) async-start(), calls=%async_computation.7 | async-start | bytes 2162688 | tf_op jit(solution)/shard_map/all_gather | solution.py:43
  251.3 65.4 %copy-start.3 = (bf16[128,256]{0,1:T(8,128)(2,1)S(1)}, bf16[128,256]{0,1:T(8,128)(2,1)}, u32[]{:S(2)}) copy-start(bf16[128,256]{0,1:T(8,128)(2,1)} %convert_element_type.23) | copy-start | bytes 196612
Sparse Core Ops, SparseCore 0:
  11.4 67.5 all-gather.4
  82.2 67.9 all-gather.8
  156.2 93.2 reduce-scatter.1
  253.8 59.2 all-gather.6
  315.3 132.9 all-gather.10
where the time goes:
time: 458 us
  waiting for transfers between devices  343 us (75%)
  blocking collectives  75 us (16%)
  between operations  13.8 us (3%)
  matrix products  12.9 us (3%)
  local copies, waits for them, and re-layouts  10.7 us (2%)
    all_gather x1, waiting for transfers between devices, local(): lax.all_gather(panel_solution, 'load', axis=1, tiled=True)  131 us
    reduce_scatter x1, waiting for transfers between devices, local(): lax.psum_scatter(lax.dot_general(block, reduced, (((0,), (0,)), ((), ()))...  92.8 us
    all_gather x1, waiting for transfers between devices, local(): lax.all_gather(forward, 'factor', axis=0, tiled=True)  61.9 us
    all_gather x1, waiting for transfers between devices, local(): lax.all_gather(regrouped, 'factor', axis=0, tiled=True)  56.7 us
    all_to_all x1, blocking collectives, local(): lax.all_to_all(update_solution, 'load', split_axis=1, concat_axis=0, tile...  38.2 us
    all_to_all x1, blocking collectives, local(): lax.all_to_all(update_factor, 'factor', split_axis=1, concat_axis=0, tile...  36.8 us
  transfers between devices with their start and end apart: 5, of which 4 were waited for; matrix products, arithmetic and copies ran while one was open for 4% of the time, Pallas kernels for 0%

commit v1 on v0

v1 whole, which is shorter than its diff:
```python
import functools

import jax
import jax.numpy as jnp
from jax import lax
from jax.experimental import pallas as pl
from jax.experimental.pallas import tpu as pltpu
from jax.sharding import PartitionSpec as P

MESH = pl.DeviceIdType.MESH
BF16 = jnp.bfloat16
F32 = jnp.float32
CHIPS = 8
ROWS = 128
COLS = 256
PIECES = 2


def kernel(
    bp, bu, pinv, uf, xs, ws, out_u, out_s, out_r,
    bp_all, f_all, red_all, p_v, pc, pt, u_v, ut, x_r, bu_v, w2, s_all,
    c_out, c_in, c_own, rs_out, rs_in, r_acc, r_in,
    loc, x_s, x_rv, ag_s, ag_r, sib_s, sib_r, p_s, p_r, w_s, w_r, c_s, c_r, rs_s, rs_r, zs, zr, r_s,
):
    f = lax.axis_index("factor")
    l = lax.axis_index("load")
    j, c = f // 2, f % 2
    h, y = j // 4, j % 4
    z, s = l // 2, l % 2
    sib = 2 * j + 1 - c

    def rdma(src, dst, ss, rs, df, dl):
        return pltpu.make_async_remote_copy(
            src_ref=src, dst_ref=dst, send_sem=ss, recv_sem=rs,
            device_id={"factor": df, "load": dl}, device_id_type=MESH,
        )

    def rows(ref, i, n=ROWS):
        return ref.at[pl.ds(pl.multiple_of(i * n, n), n)]

    def cols(ref, i, n):
        return ref.at[:, pl.ds(pl.multiple_of(i * n, n), n)]

    l_u = pltpu.make_async_copy(uf, u_v, loc.at[0])
    l_p = pltpu.make_async_copy(pinv, p_v, loc.at[1])
    l_b = pltpu.make_async_copy(bp, rows(bp_all, f), loc.at[2])
    l_x = pltpu.make_async_copy(cols(xs, l, COLS), rows(x_r, l, 16), loc.at[3])
    l_bu = pltpu.make_async_copy(bu, bu_v, loc.at[4])
    l_pc = pltpu.make_async_copy(cols(pinv, f, ROWS), pc.at[f], loc.at[5])
    for cp in (l_b, l_p, l_x, l_u, l_bu, l_pc):
        cp.start()

    def l_w(i):
        return pltpu.make_async_copy(cols(ws, 2 * i + s, COLS), w2.at[i, pl.ds(0, 96)], loc.at[6 + i])

    @pl.loop(0, 16)
    def _(i):
        l_w(i).start()

    barrier = pltpu.get_barrier_semaphore()

    def hello(df, dl):
        pl.semaphore_signal(barrier, inc=1, device_id={"factor": df, "load": dl}, device_id_type=MESH)

    @pl.loop(1, 32)
    def _(d):
        hello(f, (l + d) % 32)

    @pl.loop(1, 8)
    def _(d):
        hello(h * 8 + (f + d) % 8, l)

    @pl.loop(0, 8)
    def _(d):
        hello((1 - h) * 8 + d, 2 * z + 1 - s)

    @pl.loop(0, 4)
    def _(d):
        hello((1 - h) * 8 + 2 * d + c, l)

    pl.semaphore_wait(barrier, 31 + 7 + 8 + 4)

    def chip_copy(k, buf, d, target):
        own = rows(buf, f)
        return rdma(own, own, ag_s.at[k, d], ag_r.at[k, d], 2 * ((j + d) % CHIPS) + c, l)

    def chip_recv(k, buf, d):
        got = rows(buf, 2 * ((j + CHIPS - d) % CHIPS) + c)
        return rdma(got, got, ag_s.at[k, d], ag_r.at[k, d], sib, l)

    def core_copy(k, buf, d):
        got = rows(buf, 2 * ((j + CHIPS - d) % CHIPS) + c)
        return rdma(got, got, sib_s.at[k, d], sib_r.at[k, d], sib, l)

    def gather_start(k, buf):
        @pl.loop(1, CHIPS)
        def _(d):
            chip_copy(k, buf, d, None).start()

        core_copy(k, buf, 0).start()

    def gather_forward(k, buf):
        @pl.loop(1, CHIPS)
        def _(d):
            chip_recv(k, buf, d).wait_recv()
            core_copy(k, buf, d).start()

    def gather_finish(k, buf):
        @pl.loop(0, CHIPS)
        def _(d):
            core_copy(k, buf, d).wait_recv()

    def gather_sent(k, buf):
        @pl.loop(1, CHIPS)
        def _(d):
            chip_copy(k, buf, d, None).wait_send()

        @pl.loop(0, CHIPS)
        def _(d):
            core_copy(k, buf, d).wait_send()

    def x_copy(d):
        to = (l + d) % 32
        return rdma(cols(xs, to, COLS), rows(x_r, l, 16), x_s.at[d], x_rv.at[d], f, to)

    def x_recv(d):
        got = rows(x_r, (l + 32 - d) % 32, 16)
        return rdma(got, got, x_s.at[d], x_rv.at[d], f, l)

    l_b.wait()
    gather_start(0, bp_all)

    @pl.loop(1, 32)
    def _(d):
        x_copy(d).start()

    def p_copy(d):
        to = (f + d) % 16
        same = 1 - (to // 8 + h) % 2
        dl = 2 * z + same * s + (1 - same) * (1 - s)
        return rdma(cols(p_v, to, ROWS), pc.at[f], p_s.at[d], p_r.at[d], to, dl)

    def p_recv(d):
        got = pc.at[(f + 16 - d) % 16]
        return rdma(got, got, p_s.at[d], p_r.at[d], sib, l)

    def w_copy(i):
        zz = 8 * c + i
        return rdma(
            cols(ws, 2 * zz + 1 - s, COLS), w2.at[zz, pl.ds(96, 96)], w_s.at[i], w_r.at[i], f, 2 * z + 1 - s
        )

    def w_core(i):
        got = w2.at[8 * c + i, pl.ds(96, 96)]
        return rdma(got, got, w_s.at[8 + i], w_r.at[8 + i], sib, l)

    def w_core_recv(i):
        got = w2.at[8 * (1 - c) + i, pl.ds(96, 96)]
        return rdma(got, got, w_s.at[8 + i], w_r.at[8 + i], sib, l)

    l_p.wait()
    gather_forward(0, bp_all)

    @pl.loop(1, 16)
    def _(d):
        p_copy(d).start()

    gather_finish(0, bp_all)
    fwd = jnp.dot(p_v[...], bp_all[...], preferred_element_type=F32).astype(BF16)
    f_all[pl.ds(pl.multiple_of(f * ROWS, ROWS), ROWS), :] = fwd
    gather_start(1, f_all)

    @pl.loop(0, 8)
    def _(i):
        w_copy(i).start()

    l_u.wait()

    @pl.loop(0, 16)
    def _(i):
        at = pl.ds(pl.multiple_of(i * ROWS, ROWS), ROWS)
        ut[at, :] = u_v[:, at].T

    gather_forward(1, f_all)

    l_x.wait()

    @pl.loop(1, 32)
    def _(d):
        x_recv(d).wait_recv()

    def c_copy(i):
        return rdma(c_out.at[i], c_in.at[i], c_s.at[i], c_r.at[i], sib, l)

    def partial(i, core):
        at = pl.ds(pl.multiple_of((2 * i + core) * ROWS, ROWS), ROWS)
        return jnp.dot(ut[at, :], x_r[...], preferred_element_type=F32)

    @pl.loop(0, CHIPS)
    def _(i):
        c_out[i] = partial(i, 1 - c).astype(BF16)
        c_copy(i).start()

    @pl.loop(0, CHIPS)
    def _(i):
        c_own[i] = partial(i, c)

    def rs_copy(d):
        to = (j + d) % CHIPS
        return rdma(rs_out.at[to], rs_in.at[d], rs_s.at[d], rs_r.at[d], 2 * to + c, l)

    @pl.loop(1, CHIPS)
    def _(d):
        to = (j + d) % CHIPS
        c_copy(to).wait_recv()
        rs_out[to] = (c_own[to] + c_in[to].astype(F32)).astype(BF16)
        rs_copy(d).start()

    c_copy(j).wait_recv()
    c_own[j] = c_own[j] + c_in[j].astype(F32)

    gather_finish(1, f_all)
    l_bu.wait()

    @pl.loop(0, 4)
    def _(i):
        at = pl.ds(pl.multiple_of(i * ROWS, ROWS), ROWS)
        low = jnp.dot(u_v[at, :], f_all[...], preferred_element_type=F32)
        bu_v[at, :] = (bu_v[at, :].astype(F32) - low).astype(BF16)

    o_u = pltpu.make_async_copy(bu_v, out_u, loc.at[22])
    o_u.start()

    @pl.loop(1, CHIPS)
    def _(d):
        rs_copy(d).wait_recv()
        c_own[j] = c_own[j] + rs_in[d].astype(F32)

    mine = pl.ds(pl.multiple_of(f * ROWS, ROWS), ROWS)
    red_all[mine, :] = (f_all[mine, :].astype(F32) - c_own[j]).astype(BF16)
    gather_start(2, red_all)

    l_pc.wait()

    @pl.loop(1, 16)
    def _(d):
        p_recv(d).wait_recv()

    @pl.loop(0, 16)
    def _(i):
        at = pl.ds(pl.multiple_of(i * ROWS, ROWS), ROWS)
        pt[:, at] = pc[i].T

    gather_forward(2, red_all)

    @pl.loop(0, 8)
    def _(i):
        w_copy(i).wait_recv()
        w_core(i).start()

    gather_finish(2, red_all)
    sol = jnp.dot(pt[...], red_all[...], preferred_element_type=F32).astype(BF16)
    s_all[z] = sol
    o_s = pltpu.make_async_copy(s_all.at[z], out_s, loc.at[23])
    o_s.start()

    def piece(i, q):
        n = ROWS // PIECES
        return s_all.at[i, pl.ds(pl.multiple_of(q * n, n), n)]

    def up(t, q):
        it = piece((z + 16 - t) % 16, q)
        return rdma(it, it, zs.at[0, t, q], zr.at[0, t, q], f, (l + 2) % 32)

    def up_recv(t, q):
        it = piece((z + 15 - t) % 16, q)
        return rdma(it, it, zs.at[0, t, q], zr.at[0, t, q], sib, l)

    def down(t, q):
        it = piece((z + t) % 16, q)
        return rdma(it, it, zs.at[1, t, q], zr.at[1, t, q], f, (l + 30) % 32)

    def down_recv(t, q):
        it = piece((z + t + 1) % 16, q)
        return rdma(it, it, zs.at[1, t, q], zr.at[1, t, q], sib, l)

    def product(i):
        return lax.dot_general(w2[i], s_all[i], (((1,), (1,)), ((), ())), preferred_element_type=F32)

    for q in range(PIECES):
        up(0, q).start()
        down(0, q).start()

    @pl.loop(0, 16)
    def _(i):
        l_w(i).wait()

    @pl.loop(0, 8)
    def _(i):
        w_core_recv(i).wait_recv()

    r_acc[...] = product(z)

    @pl.loop(1, 7)
    def _(t):
        for q in range(PIECES):
            up_recv(t - 1, q).wait_recv()
            up(t, q).start()
            down_recv(t - 1, q).wait_recv()
            down(t, q).start()
        r_acc[...] += product((z + 16 - t) % 16) + product((z + t) % 16)

    for q in range(PIECES):
        up_recv(6, q).wait_recv()
        up(7, q).start()
    r_acc[...] += product((z + 9) % 16)
    for q in range(PIECES):
        down_recv(6, q).wait_recv()
    r_acc[...] += product((z + 7) % 16)
    for q in range(PIECES):
        up_recv(7, q).wait_recv()
    r_acc[...] += product((z + 8) % 16)

    swap = rdma(r_acc.at[pl.ds(96, 96)], r_in, r_s.at[0], r_s.at[1], f, 2 * z + 1 - s)
    swap.start()

    for k, buf in enumerate((bp_all, f_all, red_all)):
        gather_sent(k, buf)

    @pl.loop(1, 32)
    def _(d):
        x_copy(d).wait_send()

    @pl.loop(1, 16)
    def _(d):
        p_copy(d).wait_send()

    @pl.loop(0, 8)
    def _(i):
        w_copy(i).wait_send()
        w_core(i).wait_send()
        c_copy(i).wait_send()

    @pl.loop(1, CHIPS)
    def _(d):
        rs_copy(d).wait_send()

    @pl.loop(0, 7)
    def _(t):
        for q in range(PIECES):
            up(t, q).wait_send()
            down(t, q).wait_send()

    for q in range(PIECES):
        up(7, q).wait_send()
    o_u.wait()
    o_s.wait()
    swap.wait()
    r_in[...] = r_acc[pl.ds(0, 96), :] + r_in[...]
    o_r = pltpu.make_async_copy(r_in, out_r, loc.at[24])
    o_r.start()
    o_r.wait()


def local(bp, bu, pinv, uf, xs, ws):
    dma = pltpu.SemaphoreType.DMA
    vm = pltpu.VMEM
    hbm = pl.BlockSpec(memory_space=pl.ANY)
    return pl.pallas_call(
        kernel,
        name="solves",
        out_shape=(
            jax.ShapeDtypeStruct((512, COLS), BF16),
            jax.ShapeDtypeStruct((ROWS, COLS), BF16),
            jax.ShapeDtypeStruct((96, ROWS), F32),
        ),
        in_specs=[hbm] * 6,
        out_specs=(hbm,) * 3,
        scratch_shapes=[
            vm((2048, COLS), BF16), vm((2048, COLS), BF16), vm((2048, COLS), BF16),
            vm((ROWS, 2048), BF16), vm((16, ROWS, ROWS), BF16), vm((ROWS, 2048), BF16),
            vm((512, 2048), BF16), vm((2048, 512), BF16), vm((512, COLS), BF16), vm((512, COLS), BF16),
            vm((16, 192, COLS), BF16), vm((16, ROWS, COLS), BF16),
            vm((CHIPS, ROWS, COLS), BF16), vm((CHIPS, ROWS, COLS), BF16), vm((CHIPS, ROWS, COLS), F32),
            vm((CHIPS, ROWS, COLS), BF16), vm((CHIPS, ROWS, COLS), BF16),
            vm((192, ROWS), F32), vm((96, ROWS), F32),
            dma((25,)), dma((32,)), dma((32,)), dma((3, 8)), dma((3, 8)), dma((3, 8)), dma((3, 8)),
            dma((16,)), dma((16,)), dma((16,)), dma((16,)), dma((8,)), dma((8,)), dma((8,)), dma((8,)),
            dma((2, 8, PIECES)), dma((2, 8, PIECES)), dma((2,)),
        ],
        compiler_params=pltpu.CompilerParams(
            collective_id=0, has_side_effects=True, vmem_limit_bytes=56 << 20
        ),
    )(bp, bu, pinv, uf, xs, ws)


def solution(mesh):
    in_specs = (
        P("factor", "load"),
        P("factor", "load"),
        P("factor", None),
        P("factor", None),
        P(("factor", "load"), None),
        P("load", None),
    )
    out_specs = (P("factor", "load"), P("factor", "load"), P("load", "factor"))
    return jax.shard_map(local, mesh=mesh, in_specs=in_specs, out_specs=out_specs, check_vma=False)
```

time: 458 us -> 98.7 us (0.22)
  the two profiles are of different devices: /device:TPU:24 before, /device:TPU:32 now
where the time goes in v1:
time: 98.7 us; the launch traced here: 98.5 us
  Pallas kernels  93.3 us (95%)
  local copies, waits for them, and re-layouts  4.56 us (5%)
    pallas_call x1, Pallas kernels, local(): pl.pallas_call(kernel, name='solves', out_shape=(jax.ShapeDtypeStruct((51...  93.3 us
    unnamed x3, local copies, waits for them, and re-layouts  4.56 us

profile of v1, /device:TPU:32, one launch (start us, length us, event | category | flops | bytes accessed | tf_op | source)
XLA Modules:
  0.0 98.5 jit_solution(15730575643928041055)
XLA Ops:
  0.6 93.3 %solves.1 = (bf16[512,256]{1,0:T(8,128)(2,1)}, bf16[128,256]{1,0:T(8,128)(2,1)}, f32[96,128]{1,0:T(8,128)}) custom-call(bf16[128,256]{1,0:T(8,128)(2,1)} %bp.1, bf16[512,256]{1,0:T(8,128)(2,1)} %bu.1, bf16[128,2048]{1,0:T(8,128)(2,1)} %pinv.1, bf16[512,2048]{1,0:T(8,128)(2,1)} %uf.1, bf16[16,8192]{1,0:T(8,128)(2,1)} %xs.1, bf16[96,8192]{1,0:T(8,128)(2,1)} %ws.1), custom_call_target="tpu_custom_call" | custom-call | tf_op jit(solution)/shard_map/solves/pallas_call | solution.py:369
  93.9 1.7 %copy.12 = bf16[512,256]{1,0:T(8,128)(2,1)} copy(bf16[512,256]{1,0:T(8,128)(2,1)} %get-tuple-element.6) | data formatting | bytes 524288
  95.6 1.5 %copy.13 = bf16[128,256]{1,0:T(8,128)(2,1)} copy(bf16[128,256]{1,0:T(8,128)(2,1)} %get-tuple-element.7) | data formatting | bytes 131072
  97.0 1.4 %copy.14 = f32[96,128]{1,0:T(8,128)} copy(f32[96,128]{1,0:T(8,128)} %get-tuple-element.8) | data formatting | bytes 98304

commit v2 on v1

v2 whole, which is shorter than its diff:
```python
import functools

import jax
import jax.numpy as jnp
from jax import lax
from jax.experimental import pallas as pl
from jax.experimental.pallas import tpu as pltpu
from jax.sharding import PartitionSpec as P

MESH = pl.DeviceIdType.MESH
BF16 = jnp.bfloat16
F32 = jnp.float32
CHIPS = 8
ROWS = 128
COLS = 256


def kernel(
    bp, bu, pinv, uf, xs, ws, out_u, out_s, out_r,
    bp_all, f_all, red_all, p_v, pc, pt, u_v, ut, x_r, bu_v, w2, s_all,
    c_out, c_in, c_own, rs_out, rs_in, r_acc, r_in,
    loc, x_s, x_rv, ag_s, ag_r, sib_s, sib_r, p_s, p_r, w_s, w_r, c_s, c_r, rs_s, rs_r, fs, fr, ns, nr, r_s,
):
    f = lax.axis_index("factor")
    l = lax.axis_index("load")
    j, c = f // 2, f % 2
    h, y = j // 4, j % 4
    z, s = l // 2, l % 2
    sib = 2 * j + 1 - c

    pending = {}

    def settle(name):
        pending.pop(name)()

    def later(name, copy, lo, hi, how):
        def run():
            @pl.loop(lo, hi)
            def _(i):
                getattr(copy(i), how)()

        pending[name] = run

    def rdma(src, dst, ss, rs, df, dl):
        return pltpu.make_async_remote_copy(
            src_ref=src, dst_ref=dst, send_sem=ss, recv_sem=rs,
            device_id={"factor": df, "load": dl}, device_id_type=MESH,
        )

    def rows(ref, i, n=ROWS):
        return ref.at[pl.ds(pl.multiple_of(i * n, n), n)]

    def cols(ref, i, n):
        return ref.at[:, pl.ds(pl.multiple_of(i * n, n), n)]

    l_u = pltpu.make_async_copy(uf, u_v, loc.at[0])
    l_p = pltpu.make_async_copy(pinv, p_v, loc.at[1])
    l_b = pltpu.make_async_copy(bp, rows(bp_all, f), loc.at[2])
    l_x = pltpu.make_async_copy(cols(xs, l, COLS), rows(x_r, l, 16), loc.at[3])
    l_bu = pltpu.make_async_copy(bu, bu_v, loc.at[4])
    l_pc = pltpu.make_async_copy(cols(pinv, f, ROWS), pc.at[f], loc.at[5])
    for at, cp in enumerate((l_b, l_p, l_x, l_u, l_bu, l_pc)):
        cp.start()
        pending["l%d" % at] = cp.wait

    def l_w(i):
        return pltpu.make_async_copy(cols(ws, 2 * i + s, COLS), w2.at[i, pl.ds(0, 96)], loc.at[6 + i])

    @pl.loop(0, 16)
    def _(i):
        l_w(i).start()

    later("w own", l_w, 0, 16, "wait")

    barrier = pltpu.get_barrier_semaphore()

    def hello(df, dl):
        pl.semaphore_signal(barrier, inc=1, device_id={"factor": df, "load": dl}, device_id_type=MESH)

    @pl.loop(1, 32)
    def _(d):
        hello(f, (l + d) % 32)

    @pl.loop(1, 8)
    def _(d):
        hello(h * 8 + (f + d) % 8, l)

    @pl.loop(0, 8)
    def _(d):
        hello((1 - h) * 8 + d, 2 * z + 1 - s)

    @pl.loop(0, 4)
    def _(d):
        hello((1 - h) * 8 + 2 * d + c, l)

    pl.semaphore_wait(barrier, 31 + 7 + 8 + 4)

    def chip_copy(k, buf, d):
        own = rows(buf, f)
        return rdma(own, own, ag_s.at[k, d], ag_r.at[k, d], 2 * ((j + d) % CHIPS) + c, l)

    def chip_recv(k, buf, d):
        got = rows(buf, 2 * ((j + CHIPS - d) % CHIPS) + c)
        return rdma(got, got, ag_s.at[k, d], ag_r.at[k, d], sib, l)

    def core_copy(k, buf, d):
        got = rows(buf, 2 * ((j + CHIPS - d) % CHIPS) + c)
        return rdma(got, got, sib_s.at[k, d], sib_r.at[k, d], sib, l)

    def gather_start(k, buf):
        @pl.loop(1, CHIPS)
        def _(d):
            chip_copy(k, buf, d).start()

        core_copy(k, buf, 0).start()
        later(("chips sent", k), lambda d: chip_copy(k, buf, d), 1, CHIPS, "wait_send")
        later(("cores sent", k), lambda d: core_copy(k, buf, d), 0, CHIPS, "wait_send")
        later(("cores", k), lambda d: core_copy(k, buf, d), 0, CHIPS, "wait_recv")

    def gather_forward(k, buf):
        @pl.loop(1, CHIPS)
        def _(d):
            chip_recv(k, buf, d).wait_recv()
            core_copy(k, buf, d).start()

    def x_copy(d):
        to = (l + d) % 32
        return rdma(cols(xs, to, COLS), rows(x_r, l, 16), x_s.at[d], x_rv.at[d], f, to)

    def x_recv(d):
        got = rows(x_r, (l + 32 - d) % 32, 16)
        return rdma(got, got, x_s.at[d], x_rv.at[d], f, l)

    settle("l0")
    gather_start(0, bp_all)

    @pl.loop(1, 32)
    def _(d):
        x_copy(d).start()

    later("x sent", x_copy, 1, 32, "wait_send")
    later("x", x_recv, 1, 32, "wait_recv")

    def p_copy(d):
        to = (f + d) % 16
        same = 1 - (to // 8 + h) % 2
        dl = 2 * z + same * s + (1 - same) * (1 - s)
        return rdma(cols(p_v, to, ROWS), pc.at[f], p_s.at[d], p_r.at[d], to, dl)

    def p_recv(d):
        got = pc.at[(f + 16 - d) % 16]
        return rdma(got, got, p_s.at[d], p_r.at[d], sib, l)

    def w_copy(i):
        zz = 8 * c + i
        return rdma(
            cols(ws, 2 * zz + 1 - s, COLS), w2.at[zz, pl.ds(96, 96)], w_s.at[i], w_r.at[i], f, 2 * z + 1 - s
        )

    def w_core(i):
        got = w2.at[8 * c + i, pl.ds(96, 96)]
        return rdma(got, got, w_s.at[8 + i], w_r.at[8 + i], sib, l)

    def w_core_recv(i):
        got = w2.at[8 * (1 - c) + i, pl.ds(96, 96)]
        return rdma(got, got, w_s.at[8 + i], w_r.at[8 + i], sib, l)

    settle("l1")

    @pl.loop(1, 16)
    def _(d):
        p_copy(d).start()

    later("p sent", p_copy, 1, 16, "wait_send")
    later("p", p_recv, 1, 16, "wait_recv")

    @pl.loop(0, 8)
    def _(i):
        w_copy(i).start()

    later("w sent", w_copy, 0, 8, "wait_send")
    later("w", w_copy, 0, 8, "wait_recv")

    gather_forward(0, bp_all)

    settle(("cores", 0))
    fwd = jnp.dot(p_v[...], bp_all[...], preferred_element_type=F32).astype(BF16)
    f_all[pl.ds(pl.multiple_of(f * ROWS, ROWS), ROWS), :] = fwd

    settle("l3")

    @pl.loop(0, 16)
    def _(i):
        at = pl.ds(pl.multiple_of(i * ROWS, ROWS), ROWS)
        ut[at, :] = u_v[:, at].T

    settle("l2")

    settle("x")

    def c_copy(i):
        return rdma(c_out.at[i], c_in.at[i], c_s.at[i], c_r.at[i], sib, l)

    def partial(i, core):
        at = pl.ds(pl.multiple_of((2 * i + core) * ROWS, ROWS), ROWS)
        return jnp.dot(ut[at, :], x_r[...], preferred_element_type=F32)

    @pl.loop(0, CHIPS)
    def _(i):
        c_out[i] = partial(i, 1 - c).astype(BF16)
        c_copy(i).start()

    later("c sent", c_copy, 0, CHIPS, "wait_send")

    @pl.loop(0, CHIPS)
    def _(i):
        c_own[i] = partial(i, c)

    def rs_copy(d):
        to = (j + d) % CHIPS
        return rdma(rs_out.at[to], rs_in.at[d], rs_s.at[d], rs_r.at[d], 2 * to + c, l)

    @pl.loop(1, CHIPS)
    def _(d):
        to = (j + d) % CHIPS
        c_copy(to).wait_recv()
        rs_out[to] = (c_own[to] + c_in[to].astype(F32)).astype(BF16)
        rs_copy(d).start()

    later("rs sent", rs_copy, 1, CHIPS, "wait_send")
    c_copy(j).wait_recv()
    c_own[j] = c_own[j] + c_in[j].astype(F32)

    @pl.loop(1, CHIPS)
    def _(d):
        rs_copy(d).wait_recv()
        c_own[j] = c_own[j] + rs_in[d].astype(F32)

    mine = pl.ds(pl.multiple_of(f * ROWS, ROWS), ROWS)
    red_all[mine, :] = (f_all[mine, :].astype(F32) - c_own[j]).astype(BF16)
    gather_start(2, red_all)

    settle("l5")

    settle("p")

    @pl.loop(0, 16)
    def _(i):
        at = pl.ds(pl.multiple_of(i * ROWS, ROWS), ROWS)
        pt[:, at] = pc[i].T

    gather_forward(2, red_all)

    settle("w")

    @pl.loop(0, 8)
    def _(i):
        w_core(i).start()

    later("w core sent", w_core, 0, 8, "wait_send")
    later("w core", w_core_recv, 0, 8, "wait_recv")

    settle(("cores", 2))
    sol = jnp.dot(pt[...], red_all[...], preferred_element_type=F32).astype(BF16)
    s_all[z] = sol
    o_s = pltpu.make_async_copy(s_all.at[z], out_s, loc.at[23])
    o_s.start()

    HALF = ROWS // 2
    legs = ((0, 1), (1, -1), (1, 1), (0, -1))

    def half(i, q):
        return s_all.at[i, pl.ds(q * HALF, HALF)]

    def last(q, way):
        return 4 if way == (1 - 2 * q) else 3

    def far(q, way, k):
        it = half((z + 32 - way * 2 * k) % 16, q)
        at = (q, (1 - way) // 2, k)
        return rdma(it, it, fs.at[at], fr.at[at], f, (l + 64 + 4 * way) % 32)

    def far_recv(q, way, k):
        it = half((z + 32 - way * (2 * k + 2)) % 16, q)
        at = (q, (1 - way) // 2, k)
        return rdma(it, it, fs.at[at], fr.at[at], sib, l)

    def near(q, way, k):
        it = half((z + 32 - way * 2 * k) % 16, q)
        at = (q, (1 - way) // 2, k)
        return rdma(it, it, ns.at[at], nr.at[at], f, (l + 64 + 2 * way) % 32)

    def near_recv(q, way, k):
        it = half((z + 32 - way * (2 * k + 1)) % 16, q)
        at = (q, (1 - way) // 2, k)
        return rdma(it, it, ns.at[at], nr.at[at], sib, l)

    def product(i):
        return lax.dot_general(w2[i % 16], s_all[i % 16], (((1,), (1,)), ((), ())), preferred_element_type=F32)

    for q, way in legs:
        far(q, way, 0).start()
    for q, way in legs:
        near(q, way, 0).start()
        later(("far sent", q, way), lambda k, q=q, way=way: far(q, way, k), 0, last(q, way), "wait_send")
        later(("near sent", q, way), lambda k, q=q, way=way: near(q, way, k), 0, 4, "wait_send")
    gather_start(1, f_all)
    settle("w own")
    settle("w core")
    r_acc[...] = product(z)
    for k in range(1, 4):
        for q, way in legs:
            far_recv(q, way, k - 1).wait_recv()
            if k < last(q, way):
                far(q, way, k).start()
        for q, way in legs:
            near(q, way, k).start()
        if k == 3:
            gather_forward(1, f_all)
        r_acc[...] += product(z + 2 * k) + product(z + 16 - 2 * k)
        for q, way in legs:
            near_recv(q, way, k - 1).wait_recv()
        r_acc[...] += product(z + 2 * k - 1) + product(z + 17 - 2 * k)

    settle(("cores", 1))
    settle("l4")

    @pl.loop(0, 4)
    def _(i):
        at = pl.ds(pl.multiple_of(i * ROWS, ROWS), ROWS)
        low = jnp.dot(u_v[at, :], f_all[...], preferred_element_type=F32)
        bu_v[at, :] = (bu_v[at, :].astype(F32) - low).astype(BF16)

    o_u = pltpu.make_async_copy(bu_v, out_u, loc.at[22])
    o_u.start()

    for q, way in legs:
        near_recv(q, way, 3).wait_recv()
    r_acc[...] += product(z + 7) + product(z + 9)
    for q, way in legs[:2]:
        far_recv(q, way, 3).wait_recv()
    r_acc[...] += product(z + 8)

    swap = rdma(r_acc.at[pl.ds(96, 96)], r_in, r_s.at[0], r_s.at[1], f, 2 * z + 1 - s)
    swap.start()

    for name in list(pending):
        settle(name)
    o_u.wait()
    o_s.wait()
    swap.wait()
    r_in[...] = r_acc[pl.ds(0, 96), :] + r_in[...]
    o_r = pltpu.make_async_copy(r_in, out_r, loc.at[24])
    o_r.start()
    o_r.wait()


def leave(u, s, r, out_u, out_s, out_r):
    out_u[...] = u[...]
    out_s[...] = s[...]
    out_r[...] = r[...]


def local(bp, bu, pinv, uf, xs, ws):
    dma = pltpu.SemaphoreType.DMA
    vm = pltpu.VMEM
    hbm = pl.BlockSpec(memory_space=pl.ANY)
    outs = (
        jax.ShapeDtypeStruct((512, COLS), BF16),
        jax.ShapeDtypeStruct((ROWS, COLS), BF16),
        jax.ShapeDtypeStruct((96, ROWS), F32),
    )
    results = pl.pallas_call(
        kernel,
        name="solves",
        out_shape=outs,
        in_specs=[hbm] * 6,
        out_specs=(hbm,) * 3,
        scratch_shapes=[
            vm((2048, COLS), BF16), vm((2048, COLS), BF16), vm((2048, COLS), BF16),
            vm((ROWS, 2048), BF16), vm((16, ROWS, ROWS), BF16), vm((ROWS, 2048), BF16),
            vm((512, 2048), BF16), vm((2048, 512), BF16), vm((512, COLS), BF16), vm((512, COLS), BF16),
            vm((16, 192, COLS), BF16), vm((16, ROWS, COLS), BF16),
            vm((CHIPS, ROWS, COLS), BF16), vm((CHIPS, ROWS, COLS), BF16), vm((CHIPS, ROWS, COLS), F32),
            vm((CHIPS, ROWS, COLS), BF16), vm((CHIPS, ROWS, COLS), BF16),
            vm((192, ROWS), F32), vm((96, ROWS), F32),
            dma((25,)), dma((32,)), dma((32,)), dma((3, 8)), dma((3, 8)), dma((3, 8)), dma((3, 8)),
            dma((16,)), dma((16,)), dma((16,)), dma((16,)), dma((8,)), dma((8,)), dma((8,)), dma((8,)),
            dma((2, 2, 4)), dma((2, 2, 4)), dma((2, 2, 4)), dma((2, 2, 4)), dma((2,)),
        ],
        compiler_params=pltpu.CompilerParams(
            collective_id=0, has_side_effects=True, vmem_limit_bytes=56 << 20
        ),
    )(bp, bu, pinv, uf, xs, ws)
    return pl.pallas_call(
        leave,
        name="leave",
        out_shape=outs,
        in_specs=[pl.BlockSpec(memory_space=vm)] * 3,
        out_specs=(pl.BlockSpec(memory_space=vm),) * 3,
    )(*results)


def solution(mesh):
    in_specs = (
        P("factor", "load"),
        P("factor", "load"),
        P("factor", None),
        P("factor", None),
        P(("factor", "load"), None),
        P("load", None),
    )
    out_specs = (P("factor", "load"), P("factor", "load"), P("load", "factor"))
    return jax.shard_map(local, mesh=mesh, in_specs=in_specs, out_specs=out_specs, check_vma=False)
```

time: 98.7 us -> 82.1 us (0.83)
  the two profiles are of different devices: /device:TPU:32 before, /device:TPU:2 now
where the time goes in v2:
time: 82.1 us; the launch traced here: 81.9 us
  Pallas kernels  81.3 us (99%)
    pallas_call x1, Pallas kernels, local(): pl.pallas_call(kernel, name='solves', out_shape=outs, in_specs=[hbm] * 6,...  79.6 us
    pallas_call x1, Pallas kernels, local(): pl.pallas_call(leave, name='leave', out_shape=outs, in_specs=[pl.BlockSpe...  1.73 us

profile of v2, /device:TPU:2, one launch (start us, length us, event | category | flops | bytes accessed | tf_op | source)
XLA Modules:
  0.0 81.9 jit_solution(3473739558383611535)
XLA Ops:
  0.6 79.6 %solves.1 = (bf16[512,256]{1,0:T(8,128)(2,1)}, bf16[128,256]{1,0:T(8,128)(2,1)}, f32[96,128]{1,0:T(8,128)}) custom-call(bf16[128,256]{1,0:T(8,128)(2,1)} %bp.1, bf16[512,256]{1,0:T(8,128)(2,1)} %bu.1, bf16[128,2048]{1,0:T(8,128)(2,1)} %pinv.1, bf16[512,2048]{1,0:T(8,128)(2,1)} %uf.1, bf16[16,8192]{1,0:T(8,128)(2,1)} %xs.1, bf16[96,8192]{1,0:T(8,128)(2,1)} %ws.1), custom_call_target="tpu_custom_call" | custom-call | tf_op jit(solution)/shard_map/solves/pallas_call | solution.py:373
  80.2 1.7 %leave.1 = (bf16[512,256]{1,0:T(8,128)(2,1)}, bf16[128,256]{1,0:T(8,128)(2,1)}, f32[96,128]{1,0:T(8,128)}) custom-call(bf16[512,256]{1,0:T(8,128)(2,1)} %get-tuple-element.6.u, bf16[128,256]{1,0:T(8,128)(2,1)} %get-tuple-element.7.s, f32[96,128]{1,0:T(8,128)} %get-tuple-element.8.r), custom_call_target="tpu_custom_call" | custom-call | tf_op jit(solution)/shard_map/leave/pallas_call | solution.py:395

commit v3 on v2

--- a/solution.py
+++ b/solution.py
@@ -17,8 +17,8 @@
 
 def kernel(
     bp, bu, pinv, uf, xs, ws, out_u, out_s, out_r,
-    bp_all, f_all, red_all, p_v, pc, pt, u_v, ut, x_r, bu_v, w2, s_all,
-    c_out, c_in, c_own, rs_out, rs_in, r_acc, r_in,
+    bp_all, f_all, red_all, p_v, pc, pt, u_v, ut, x_r, bu_v, w2, z_all, s_v, t_all,
+    c_out, c_in, c_own, rs_out, rs_in, r_acc, r_in, r_sum,
     loc, x_s, x_rv, ag_s, ag_r, sib_s, sib_r, p_s, p_r, w_s, w_r, c_s, c_r, rs_s, rs_r, fs, fr, ns, nr, r_s,
 ):
     f = lax.axis_index("factor")
@@ -95,16 +95,18 @@
 
     pl.semaphore_wait(barrier, 31 + 7 + 8 + 4)
 
+    size = (ROWS, ROWS, ROWS, 96)
+
     def chip_copy(k, buf, d):
-        own = rows(buf, f)
+        own = rows(buf, f, size[k])
         return rdma(own, own, ag_s.at[k, d], ag_r.at[k, d], 2 * ((j + d) % CHIPS) + c, l)
 
     def chip_recv(k, buf, d):
-        got = rows(buf, 2 * ((j + CHIPS - d) % CHIPS) + c)
+        got = rows(buf, 2 * ((j + CHIPS - d) % CHIPS) + c, size[k])
         return rdma(got, got, ag_s.at[k, d], ag_r.at[k, d], sib, l)
 
     def core_copy(k, buf, d):
-        got = rows(buf, 2 * ((j + CHIPS - d) % CHIPS) + c)
+        got = rows(buf, 2 * ((j + CHIPS - d) % CHIPS) + c, size[k])
         return rdma(got, got, sib_s.at[k, d], sib_r.at[k, d], sib, l)
 
     def gather_start(k, buf):
@@ -231,46 +233,39 @@
     c_copy(j).wait_recv()
     c_own[j] = c_own[j] + c_in[j].astype(F32)
 
+    settle("l5")
+
+    settle("p")
+
+    @pl.loop(0, 16)
+    def _(i):
+        at = pl.ds(pl.multiple_of(i * ROWS, ROWS), ROWS)
+        pt[:, at] = pc[i].T
+
+    settle("w")
+
+    @pl.loop(0, 8)
+    def _(i):
+        w_core(i).start()
+
+    later("w core sent", w_core, 0, 8, "wait_send")
+    later("w core", w_core_recv, 0, 8, "wait_recv")
+
     @pl.loop(1, CHIPS)
     def _(d):
         rs_copy(d).wait_recv()
         c_own[j] = c_own[j] + rs_in[d].astype(F32)
 
     mine = pl.ds(pl.multiple_of(f * ROWS, ROWS), ROWS)
-    red_all[mine, :] = (f_all[mine, :].astype(F32) - c_own[j]).astype(BF16)
-    gather_start(2, red_all)
-
-    settle("l5")
-
-    settle("p")
-
-    @pl.loop(0, 16)
-    def _(i):
-        at = pl.ds(pl.multiple_of(i * ROWS, ROWS), ROWS)
-        pt[:, at] = pc[i].T
-
-    gather_forward(2, red_all)
-
-    settle("w")
-
-    @pl.loop(0, 8)
-    def _(i):
-        w_core(i).start()
-
-    later("w core sent", w_core, 0, 8, "wait_send")
-    later("w core", w_core_recv, 0, 8, "wait_recv")
-
-    settle(("cores", 2))
-    sol = jnp.dot(pt[...], red_all[...], preferred_element_type=F32).astype(BF16)
-    s_all[z] = sol
-    o_s = pltpu.make_async_copy(s_all.at[z], out_s, loc.at[23])
-    o_s.start()
+    red = (f_all[mine, :].astype(F32) - c_own[j]).astype(BF16)
+    z_all[z] = red
+    red_all[mine, :] = red
 
     HALF = ROWS // 2
     legs = ((0, 1), (1, -1), (1, 1), (0, -1))
 
     def half(i, q):
-        return s_all.at[i, pl.ds(q * HALF, HALF)]
+        return z_all.at[i, pl.ds(q * HALF, HALF)]
 
     def last(q, way):
         return 4 if way == (1 - 2 * q) else 3
@@ -296,7 +291,7 @@
         return rdma(it, it, ns.at[at], nr.at[at], sib, l)
 
     def product(i):
-        return lax.dot_general(w2[i % 16], s_all[i % 16], (((1,), (1,)), ((), ())), preferred_element_type=F32)
+        return lax.dot_general(w2[i % 16], z_all[i % 16], (((1,), (1,)), ((), ())), preferred_element_type=F32)
 
     for q, way in legs:
         far(q, way, 0).start()
@@ -304,7 +299,7 @@
         near(q, way, 0).start()
         later(("far sent", q, way), lambda k, q=q, way=way: far(q, way, k), 0, last(q, way), "wait_send")
         later(("near sent", q, way), lambda k, q=q, way=way: near(q, way, k), 0, 4, "wait_send")
-    gather_start(1, f_all)
+    gather_start(2, red_all)
     settle("w own")
     settle("w core")
     r_acc[...] = product(z)
@@ -315,24 +310,14 @@
                 far(q, way, k).start()
         for q, way in legs:
             near(q, way, k).start()
+        if k == 2:
+            gather_start(1, f_all)
         if k == 3:
-            gather_forward(1, f_all)
+            gather_forward(2, red_all)
         r_acc[...] += product(z + 2 * k) + product(z + 16 - 2 * k)
         for q, way in legs:
             near_recv(q, way, k - 1).wait_recv()
         r_acc[...] += product(z + 2 * k - 1) + product(z + 17 - 2 * k)
-
-    settle(("cores", 1))
-    settle("l4")
-
-    @pl.loop(0, 4)
-    def _(i):
-        at = pl.ds(pl.multiple_of(i * ROWS, ROWS), ROWS)
-        low = jnp.dot(u_v[at, :], f_all[...], preferred_element_type=F32)
-        bu_v[at, :] = (bu_v[at, :].astype(F32) - low).astype(BF16)
-
-    o_u = pltpu.make_async_copy(bu_v, out_u, loc.at[22])
-    o_u.start()
 
     for q, way in legs:
         near_recv(q, way, 3).wait_recv()
@@ -343,15 +328,45 @@
 
     swap = rdma(r_acc.at[pl.ds(96, 96)], r_in, r_s.at[0], r_s.at[1], f, 2 * z + 1 - s)
     swap.start()
+    gather_forward(1, f_all)
+    swap.wait_recv()
+    t_all[pl.ds(pl.multiple_of(f * 96, 96), 96), :] = (r_acc[pl.ds(0, 96), :] + r_in[...]).astype(BF16)
+    gather_start(3, t_all)
+
+    settle(("cores", 2))
+    s_v[...] = jnp.dot(pt[...], red_all[...], preferred_element_type=F32).astype(BF16)
+    o_s = pltpu.make_async_copy(s_v, out_s, loc.at[23])
+    o_s.start()
+    settle(("cores", 1))
+    settle("l4")
+
+    @pl.loop(0, 4)
+    def _(i):
+        at = pl.ds(pl.multiple_of(i * ROWS, ROWS), ROWS)
+        low = jnp.dot(u_v[at, :], f_all[...], preferred_element_type=F32)
+        bu_v[at, :] = (bu_v[at, :].astype(F32) - low).astype(BF16)
+
+    o_u = pltpu.make_async_copy(bu_v, out_u, loc.at[22])
+    o_u.start()
+
+    gather_forward(3, t_all)
+    settle(("cores", 3))
+    r_sum[...] = jnp.zeros((96, ROWS), F32)
+
+    @pl.loop(0, 16)
+    def _(i):
+        r_sum[...] += jnp.dot(
+            t_all[pl.ds(pl.multiple_of(i * 96, 96), 96), :], pc[i], preferred_element_type=F32
+        )
+
+    o_r = pltpu.make_async_copy(r_sum, out_r, loc.at[24])
+    o_r.start()
 
     for name in list(pending):
         settle(name)
     o_u.wait()
     o_s.wait()
-    swap.wait()
-    r_in[...] = r_acc[pl.ds(0, 96), :] + r_in[...]
-    o_r = pltpu.make_async_copy(r_in, out_r, loc.at[24])
-    o_r.start()
+    swap.wait_send()
     o_r.wait()
 
 
@@ -380,11 +395,11 @@
             vm((2048, COLS), BF16), vm((2048, COLS), BF16), vm((2048, COLS), BF16),
             vm((ROWS, 2048), BF16), vm((16, ROWS, ROWS), BF16), vm((ROWS, 2048), BF16),
             vm((512, 2048), BF16), vm((2048, 512), BF16), vm((512, COLS), BF16), vm((512, COLS), BF16),
-            vm((16, 192, COLS), BF16), vm((16, ROWS, COLS), BF16),
+            vm((16, 192, COLS), BF16), vm((16, ROWS, COLS), BF16), vm((ROWS, COLS), BF16), vm((16 * 96, ROWS), BF16),
             vm((CHIPS, ROWS, COLS), BF16), vm((CHIPS, ROWS, COLS), BF16), vm((CHIPS, ROWS, COLS), F32),
             vm((CHIPS, ROWS, COLS), BF16), vm((CHIPS, ROWS, COLS), BF16),
-            vm((192, ROWS), F32), vm((96, ROWS), F32),
-            dma((25,)), dma((32,)), dma((32,)), dma((3, 8)), dma((3, 8)), dma((3, 8)), dma((3, 8)),
+            vm((192, ROWS), F32), vm((96, ROWS), F32), vm((96, ROWS), F32),
+            dma((25,)), dma((32,)), dma((32,)), dma((4, 8)), dma((4, 8)), dma((4, 8)), dma((4, 8)),
             dma((16,)), dma((16,)), dma((16,)), dma((16,)), dma((8,)), dma((8,)), dma((8,)), dma((8,)),
             dma((2, 2, 4)), dma((2, 2, 4)), dma((2, 2, 4)), dma((2, 2, 4)), dma((2,)),
         ],

time: 82.1 us -> 83.3 us (1.015)
  the two profiles are of different devices: /device:TPU:2 before, /device:TPU:1 now
where the time goes in v3:
time: 83.3 us; the launch traced here: 83.2 us
  Pallas kernels  82.5 us (99%)
    pallas_call x1, Pallas kernels, local(): pl.pallas_call(kernel, name='solves', out_shape=outs, in_specs=[hbm] * 6,...  80.8 us
    pallas_call x1, Pallas kernels, local(): pl.pallas_call(leave, name='leave', out_shape=outs, in_specs=[pl.BlockSpe...  1.73 us

profile of v3, /device:TPU:1, one launch (start us, length us, event | category | flops | bytes accessed | tf_op | source)
XLA Modules:
  0.0 83.2 jit_solution(5788038003320900281)
XLA Ops:
  0.6 80.8 %solves.1 = (bf16[512,256]{1,0:T(8,128)(2,1)}, bf16[128,256]{1,0:T(8,128)(2,1)}, f32[96,128]{1,0:T(8,128)}) custom-call(bf16[128,256]{1,0:T(8,128)(2,1)} %bp.1, bf16[512,256]{1,0:T(8,128)(2,1)} %bu.1, bf16[128,2048]{1,0:T(8,128)(2,1)} %pinv.1, bf16[512,2048]{1,0:T(8,128)(2,1)} %uf.1, bf16[16,8192]{1,0:T(8,128)(2,1)} %xs.1, bf16[96,8192]{1,0:T(8,128)(2,1)} %ws.1), custom_call_target="tpu_custom_call" | custom-call | tf_op jit(solution)/shard_map/solves/pallas_call | solution.py:388
  81.5 1.7 %leave.1 = (bf16[512,256]{1,0:T(8,128)(2,1)}, bf16[128,256]{1,0:T(8,128)(2,1)}, f32[96,128]{1,0:T(8,128)}) custom-call(bf16[512,256]{1,0:T(8,128)(2,1)} %get-tuple-element.6.u, bf16[128,256]{1,0:T(8,128)(2,1)} %get-tuple-element.7.s, f32[96,128]{1,0:T(8,128)} %get-tuple-element.8.r), custom_call_target="tpu_custom_call" | custom-call | tf_op jit(solution)/shard_map/leave/pallas_call | solution.py:410

commit v4 on v2

--- a/solution.py
+++ b/solution.py
@@ -205,16 +205,13 @@
         at = pl.ds(pl.multiple_of((2 * i + core) * ROWS, ROWS), ROWS)
         return jnp.dot(ut[at, :], x_r[...], preferred_element_type=F32)
 
-    @pl.loop(0, CHIPS)
-    def _(i):
+    @pl.loop(1, CHIPS + 1)
+    def _(d):
+        i = (j + d) % CHIPS
         c_out[i] = partial(i, 1 - c).astype(BF16)
         c_copy(i).start()
 
     later("c sent", c_copy, 0, CHIPS, "wait_send")
-
-    @pl.loop(0, CHIPS)
-    def _(i):
-        c_own[i] = partial(i, c)
 
     def rs_copy(d):
         to = (j + d) % CHIPS
@@ -223,21 +220,23 @@
     @pl.loop(1, CHIPS)
     def _(d):
         to = (j + d) % CHIPS
+        own = partial(to, c)
         c_copy(to).wait_recv()
-        rs_out[to] = (c_own[to] + c_in[to].astype(F32)).astype(BF16)
+        rs_out[to] = (own + c_in[to].astype(F32)).astype(BF16)
         rs_copy(d).start()
 
     later("rs sent", rs_copy, 1, CHIPS, "wait_send")
+    c_own[...] = partial(j, c)
     c_copy(j).wait_recv()
-    c_own[j] = c_own[j] + c_in[j].astype(F32)
+    c_own[...] = c_own[...] + c_in[j].astype(F32)
 
     @pl.loop(1, CHIPS)
     def _(d):
         rs_copy(d).wait_recv()
-        c_own[j] = c_own[j] + rs_in[d].astype(F32)
+        c_own[...] = c_own[...] + rs_in[d].astype(F32)
 
     mine = pl.ds(pl.multiple_of(f * ROWS, ROWS), ROWS)
-    red_all[mine, :] = (f_all[mine, :].astype(F32) - c_own[j]).astype(BF16)
+    red_all[mine, :] = (f_all[mine, :].astype(F32) - c_own[...]).astype(BF16)
     gather_start(2, red_all)
 
     settle("l5")
@@ -261,11 +260,6 @@
     later("w core", w_core_recv, 0, 8, "wait_recv")
 
     settle(("cores", 2))
-    sol = jnp.dot(pt[...], red_all[...], preferred_element_type=F32).astype(BF16)
-    s_all[z] = sol
-    o_s = pltpu.make_async_copy(s_all.at[z], out_s, loc.at[23])
-    o_s.start()
-
     HALF = ROWS // 2
     legs = ((0, 1), (1, -1), (1, 1), (0, -1))
 
@@ -298,13 +292,18 @@
     def product(i):
         return lax.dot_general(w2[i % 16], s_all[i % 16], (((1,), (1,)), ((), ())), preferred_element_type=F32)
 
-    for q, way in legs:
-        far(q, way, 0).start()
+    for q in range(2):
+        part = pl.ds(q * HALF, HALF)
+        s_all[z, part, :] = jnp.dot(pt[part, :], red_all[...], preferred_element_type=F32).astype(BF16)
+        for way in (1, -1):
+            far(q, way, 0).start()
     for q, way in legs:
         near(q, way, 0).start()
         later(("far sent", q, way), lambda k, q=q, way=way: far(q, way, k), 0, last(q, way), "wait_send")
         later(("near sent", q, way), lambda k, q=q, way=way: near(q, way, k), 0, 4, "wait_send")
     gather_start(1, f_all)
+    o_s = pltpu.make_async_copy(s_all.at[z], out_s, loc.at[23])
+    o_s.start()
     settle("w own")
     settle("w core")
     r_acc[...] = product(z)
@@ -315,7 +314,12 @@
                 far(q, way, k).start()
         for q, way in legs:
             near(q, way, k).start()
+        if k == 2:
+            for name in (("chips sent", 0), ("cores sent", 0), "x sent", "p sent", "w sent", "c sent"):
+                settle(name)
         if k == 3:
+            for name in ("rs sent", "w core sent", ("chips sent", 2), ("cores sent", 2)):
+                settle(name)
             gather_forward(1, f_all)
         r_acc[...] += product(z + 2 * k) + product(z + 16 - 2 * k)
         for q, way in legs:
@@ -339,10 +343,11 @@
     r_acc[...] += product(z + 7) + product(z + 9)
     for q, way in legs[:2]:
         far_recv(q, way, 3).wait_recv()
-    r_acc[...] += product(z + 8)
-
+    tail = product(z + 8)
+    r_acc[pl.ds(96, 96), :] += tail[96:]
     swap = rdma(r_acc.at[pl.ds(96, 96)], r_in, r_s.at[0], r_s.at[1], f, 2 * z + 1 - s)
     swap.start()
+    r_acc[pl.ds(0, 96), :] += tail[:96]
 
     for name in list(pending):
         settle(name)
@@ -381,7 +386,7 @@
             vm((ROWS, 2048), BF16), vm((16, ROWS, ROWS), BF16), vm((ROWS, 2048), BF16),
             vm((512, 2048), BF16), vm((2048, 512), BF16), vm((512, COLS), BF16), vm((512, COLS), BF16),
             vm((16, 192, COLS), BF16), vm((16, ROWS, COLS), BF16),
-            vm((CHIPS, ROWS, COLS), BF16), vm((CHIPS, ROWS, COLS), BF16), vm((CHIPS, ROWS, COLS), F32),
+            vm((CHIPS, ROWS, COLS), BF16), vm((CHIPS, ROWS, COLS), BF16), vm((ROWS, COLS), F32),
             vm((CHIPS, ROWS, COLS), BF16), vm((CHIPS, ROWS, COLS), BF16),
             vm((192, ROWS), F32), vm((96, ROWS), F32),
             dma((25,)), dma((32,)), dma((32,)), dma((3, 8)), dma((3, 8)), dma((3, 8)), dma((3, 8)),

time: 82.1 us -> 83.4 us (1.016)
  Pallas kernels: 81.3 us -> 82.6 us
    pallas_call x1, Pallas kernels: 79.6 us -> 80.9 us  [local(): pl.pallas_call(kernel, name='solves', out_shape=outs, in_specs=[hbm] * 6,...]
where the time goes in v4:
time: 83.4 us; the launch traced here: 83.3 us
  Pallas kernels  82.6 us (99%)
    pallas_call x1, Pallas kernels, local(): pl.pallas_call(kernel, name='solves', out_shape=outs, in_specs=[hbm] * 6,...  80.9 us
    pallas_call x1, Pallas kernels, local(): pl.pallas_call(leave, name='leave', out_shape=outs, in_specs=[pl.BlockSpe...  1.73 us

profile of v4, /device:TPU:2, one launch (start us, length us, event | category | flops | bytes accessed | tf_op | source)
XLA Modules:
  0.0 83.3 jit_solution(9840009512939071375)
XLA Ops:
  0.6 80.9 %solves.1 = (bf16[512,256]{1,0:T(8,128)(2,1)}, bf16[128,256]{1,0:T(8,128)(2,1)}, f32[96,128]{1,0:T(8,128)}) custom-call(bf16[128,256]{1,0:T(8,128)(2,1)} %bp.1, bf16[512,256]{1,0:T(8,128)(2,1)} %bu.1, bf16[128,2048]{1,0:T(8,128)(2,1)} %pinv.1, bf16[512,2048]{1,0:T(8,128)(2,1)} %uf.1, bf16[16,8192]{1,0:T(8,128)(2,1)} %xs.1, bf16[96,8192]{1,0:T(8,128)(2,1)} %ws.1), custom_call_target="tpu_custom_call" | custom-call | tf_op jit(solution)/shard_map/solves/pallas_call | solution.py:378
  81.6 1.7 %leave.1 = (bf16[512,256]{1,0:T(8,128)(2,1)}, bf16[128,256]{1,0:T(8,128)(2,1)}, f32[96,128]{1,0:T(8,128)}) custom-call(bf16[512,256]{1,0:T(8,128)(2,1)} %get-tuple-element.6.u, bf16[128,256]{1,0:T(8,128)(2,1)} %get-tuple-element.7.s, f32[96,128]{1,0:T(8,128)} %get-tuple-element.8.r), custom_call_target="tpu_custom_call" | custom-call | tf_op jit(solution)/shard_map/leave/pallas_call | solution.py:400

commit v5 on v2

--- a/solution.py
+++ b/solution.py
@@ -77,9 +77,9 @@
     def hello(df, dl):
         pl.semaphore_signal(barrier, inc=1, device_id={"factor": df, "load": dl}, device_id_type=MESH)
 
-    @pl.loop(1, 32)
-    def _(d):
-        hello(f, (l + d) % 32)
+    @pl.loop(0, 31)
+    def _(i):
+        hello(f, (l + 16 + (i + 1) // 2 * (2 * (i % 2) - 1)) % 32)
 
     @pl.loop(1, 8)
     def _(d):

time: 82.1 us -> 82.1 us (level)
  no operation moved by 1% of the time
where the time goes in v5:
time: 82.1 us; the launch traced here: 82 us
  Pallas kernels  81.3 us (99%)
    pallas_call x1, Pallas kernels, local(): pl.pallas_call(kernel, name='solves', out_shape=outs, in_specs=[hbm] * 6,...  79.6 us
    pallas_call x1, Pallas kernels, local(): pl.pallas_call(leave, name='leave', out_shape=outs, in_specs=[pl.BlockSpe...  1.73 us

profile of v5, /device:TPU:2, one launch (start us, length us, event | category | flops | bytes accessed | tf_op | source)
XLA Modules:
  0.0 82.0 jit_solution(15166098139578658462)
XLA Ops:
  0.6 79.6 %solves.1 = (bf16[512,256]{1,0:T(8,128)(2,1)}, bf16[128,256]{1,0:T(8,128)(2,1)}, f32[96,128]{1,0:T(8,128)}) custom-call(bf16[128,256]{1,0:T(8,128)(2,1)} %bp.1, bf16[512,256]{1,0:T(8,128)(2,1)} %bu.1, bf16[128,2048]{1,0:T(8,128)(2,1)} %pinv.1, bf16[512,2048]{1,0:T(8,128)(2,1)} %uf.1, bf16[16,8192]{1,0:T(8,128)(2,1)} %xs.1, bf16[96,8192]{1,0:T(8,128)(2,1)} %ws.1), custom_call_target="tpu_custom_call" | custom-call | tf_op jit(solution)/shard_map/solves/pallas_call | solution.py:373
  80.2 1.7 %leave.1 = (bf16[512,256]{1,0:T(8,128)(2,1)}, bf16[128,256]{1,0:T(8,128)(2,1)}, f32[96,128]{1,0:T(8,128)}) custom-call(bf16[512,256]{1,0:T(8,128)(2,1)} %get-tuple-element.6.u, bf16[128,256]{1,0:T(8,128)(2,1)} %get-tuple-element.7.s, f32[96,128]{1,0:T(8,128)} %get-tuple-element.8.r), custom_call_target="tpu_custom_call" | custom-call | tf_op jit(solution)/shard_map/leave/pallas_call | solution.py:395
